TPU v7x, 32 devices: a whole 2x2x4 slice. The times are simulated.
32 devices in a mesh: dp: 2 (over y), ctx: 4 (over z), tp: 4 (over x, core).
Axes of the slice: x: 2, y: 2, z: 4, core: 2. Of those that a mesh axis runs over, the one named last changes fastest.
Arguments:
- layer_input: bfloat16 [2, 4096, 1024], P('dp', 'ctx'), may hold values from -6 to 6
- segments: int32 [2, 4096], P('dp', 'ctx'), may hold values from 0 to 16, as said below
- positions: int32 [2, 4096], P('dp', 'ctx'), may hold values from 0 to 4094, as said below
- w_q: bfloat16 [1024, 1024], P('dp', 'tp'), may hold values from -0.1875 to 0.1875
- w_k: bfloat16 [1024, 1024], P('dp', 'tp'), may hold values from -0.1875 to 0.1875
- w_v: bfloat16 [1024, 1024], P('dp', 'tp'), may hold values from -0.1875 to 0.1875
- w_o: bfloat16 [1024, 1024], P('tp', 'dp'), may hold values from -0.75 to 0.75
- w_in: bfloat16 [1024, 4096], P('dp', 'tp'), may hold values from -0.1875 to 0.1875
- w_out: bfloat16 [4096, 1024], P('tp', 'dp'), may hold values from -0.09375 to 0.09375
- ln1_gain: bfloat16 [1024], P('dp'), may hold values from 0.25 to 1.75
- ln1_bias: bfloat16 [1024], P('dp'), may hold values from -1 to 1
- ln2_gain: bfloat16 [1024], P('dp'), may hold values from 0.25 to 1.75
- ln2_bias: bfloat16 [1024], P('dp'), may hold values from -1 to 1
- cotangent: bfloat16 [2, 4096, 1024], P('dp', 'ctx'), may hold values from -6 to 6
Outputs:
- layer_output: float32 [2, 4096, 1024], P('dp', 'ctx')
- x_grad: float32 [2, 4096, 1024], P('dp', 'ctx')
- w_q_grad: float32 [1024, 1024], P('dp', 'tp')
- w_k_grad: float32 [1024, 1024], P('dp', 'tp')
- w_v_grad: float32 [1024, 1024], P('dp', 'tp')
- w_o_grad: float32 [1024, 1024], P('tp', 'dp')
- w_in_grad: float32 [1024, 4096], P('dp', 'tp')
- w_out_grad: float32 [4096, 1024], P('tp', 'dp')
- ln1_gain_grad: float32 [1024], P('dp')
- ln1_bias_grad: float32 [1024], P('dp')
- ln2_gain_grad: float32 [1024], P('dp')
- ln2_bias_grad: float32 [1024], P('dp')
Inputs may be any that keep to these rules, and one draw needn't show every extreme that they name: `segments`: along a sequence the document number never falls; it is 0 at the first slot and 16 at the last. `positions`: A slot's position is its offset from the first slot of its document.
All inputs are finite; a program needn't handle non-finite values.
Results may differ from a plain program's by a relative error of at most 0.023.
Values may be sent and summed in bfloat16 or wider, within the bound.
No kernel may reach another device: no remote copies, remote signals or barrier semaphores. Data moves between devices by JAX's collectives and lax.ppermute only.
A program may use at most 256 MiB of HBM per device.

v0:
```python
import jax
import jax.numpy as jnp
from jax import lax
from jax.sharding import PartitionSpec as P

D = 1024
H = 16
NEG_BIG = -1e30
SQRT_HALF = 0.7071067811865476
INV_SQRT_TAU = 0.3989422804014327


def rotate_heads(values, positions, head_size, sign):
    half = head_size // 2
    freq = 10000.0 ** (-jnp.arange(half, dtype=jnp.float32) * 2.0 / head_size)
    angles = positions.astype(jnp.float32)[..., None] * freq
    cosine = jnp.cos(angles)[..., None, :]
    sine = sign * jnp.sin(angles)[..., None, :]
    first = values[..., :half]
    second = values[..., half:]
    return jnp.concatenate(
        [first * cosine - second * sine, second * cosine + first * sine], axis=-1
    )


def norm_forward(values, gain, shift):
    centered = values - jnp.mean(values, axis=-1, keepdims=True)
    inverse = lax.rsqrt(jnp.mean(centered * centered, axis=-1, keepdims=True) + 1e-05)
    normed = centered * inverse
    return (normed * gain.astype(jnp.float32) + shift.astype(jnp.float32), normed, inverse)


def norm_backward(incoming, normed, inverse, gain):
    scaled = incoming * gain.astype(jnp.float32)
    inner = (
        scaled
        - jnp.mean(scaled, axis=-1, keepdims=True)
        - normed * jnp.mean(scaled * normed, axis=-1, keepdims=True)
    )
    return (inverse * inner, jnp.sum(incoming * normed, axis=0), jnp.sum(incoming, axis=0))


def body(
    layer_input,
    segments,
    positions,
    w_q,
    w_k,
    w_v,
    w_o,
    w_in,
    w_out,
    ln1_gain,
    ln1_bias,
    ln2_gain,
    ln2_bias,
    cotangent,
):
    seqs, piece_len, width = layer_input.shape
    head_size = D // H
    (
        query_weight,
        key_weight,
        value_weight,
        out_weight,
        in_weight,
        down_weight,
        gain_one,
        shift_one,
        gain_two,
        shift_two,
    ) = (
        lax.all_gather(w_q, "dp", axis=0, tiled=True),
        lax.all_gather(w_k, "dp", axis=0, tiled=True),
        lax.all_gather(w_v, "dp", axis=0, tiled=True),
        lax.all_gather(w_o, "dp", axis=1, tiled=True),
        lax.all_gather(w_in, "dp", axis=0, tiled=True),
        lax.all_gather(w_out, "dp", axis=1, tiled=True),
        lax.all_gather(ln1_gain, "dp", axis=0, tiled=True),
        lax.all_gather(ln1_bias, "dp", axis=0, tiled=True),
        lax.all_gather(ln2_gain, "dp", axis=0, tiled=True),
        lax.all_gather(ln2_bias, "dp", axis=0, tiled=True),
    )
    local_width = query_weight.shape[1]
    heads_here = local_width // head_size
    doc_whole = lax.all_gather(segments, "ctx", axis=1, tiled=True)
    full_len = doc_whole.shape[1]
    row_count = seqs * piece_len
    tokens = layer_input.reshape(row_count, width)
    scale = head_size ** (-0.5)
    doc_low = jnp.min(segments, axis=1)
    doc_high = jnp.max(segments, axis=1)
    share = row_count // lax.axis_size("tp")
    offset = lax.axis_index("tp") * share

    def reduce_heads(partial_sum):
        return lax.psum_scatter(
            partial_sum.astype(jnp.bfloat16), "tp", scatter_dimension=0, tiled=True
        ).astype(jnp.float32)

    def spread_rows(rows_low):
        return lax.all_gather(rows_low, "tp", axis=0, tiled=True)

    def own_rows(whole_rows):
        return lax.dynamic_slice_in_dim(whole_rows, offset, share, 0)

    def project(weight):
        return jnp.dot(tokens, weight, preferred_element_type=jnp.float32).reshape(
            seqs, piece_len, heads_here, head_size
        )

    queries = rotate_heads(project(query_weight), positions, head_size, 1.0).astype(jnp.bfloat16)
    keys = rotate_heads(project(key_weight), positions, head_size, 1.0).astype(jnp.bfloat16)
    values = project(value_weight).astype(jnp.bfloat16)

    def touches():
        meets = (doc_low <= jnp.max(doc_whole, axis=1)) & (jnp.min(doc_whole, axis=1) <= doc_high)
        return (jnp.any(meets), doc_whole)

    def masked_scores(key_piece, doc_keys):
        scores = (
            jnp.einsum("sqhd,skhd->shqk", queries, key_piece, preferred_element_type=jnp.float32)
            * scale
        )
        same = segments[:, None, :, None] == doc_keys[:, None, None, :]
        return jnp.where(same, scores, NEG_BIG)

    start_state = (
        jnp.full((seqs, heads_here, piece_len), NEG_BIG, jnp.float32),
        jnp.zeros((seqs, heads_here, piece_len), jnp.float32),
        jnp.zeros((seqs, piece_len, heads_here, head_size), jnp.float32),
    )
    key_piece = lax.all_gather(keys, "ctx", axis=1, tiled=True)
    value_piece = lax.all_gather(values, "ctx", axis=1, tiled=True)
    needed, doc_keys = touches()

    def forward_update(state):
        run_max, run_total, run_out = state
        scores = masked_scores(key_piece, doc_keys)
        new_max = jnp.maximum(run_max, jnp.max(scores, axis=-1))
        weights_now = jnp.exp(scores - new_max[..., None])
        factor = jnp.exp(run_max - new_max)
        new_total = jnp.sum(weights_now, axis=-1)
        added = jnp.einsum(
            "shqk,skhd->sqhd",
            weights_now.astype(jnp.bfloat16),
            value_piece,
            preferred_element_type=jnp.float32,
        )
        new_out = run_out * jnp.swapaxes(factor, 1, 2)[..., None] + added
        return (new_max, new_total, new_out)

    run_max, run_total, run_out = lax.cond(needed, forward_update, lambda state: state, start_state)
    attended = run_out / jnp.swapaxes(run_total, 1, 2)[..., None]
    log_total = run_max + jnp.log(run_total)
    attended_low = attended.astype(jnp.bfloat16).reshape(row_count, local_width)
    mixed = reduce_heads(jnp.dot(attended_low, out_weight, preferred_element_type=jnp.float32))
    token_rows = own_rows(tokens).astype(jnp.float32)
    hidden_one, normed_one, inverse_one = norm_forward(token_rows + mixed, gain_one, shift_one)
    hidden_low = spread_rows(hidden_one.astype(jnp.bfloat16))
    pre_act = jnp.dot(hidden_low, in_weight, preferred_element_type=jnp.float32)
    activated = jax.nn.gelu(pre_act, approximate=False).astype(jnp.bfloat16)
    branch_two = reduce_heads(jnp.dot(activated, down_weight, preferred_element_type=jnp.float32))
    output, normed_two, inverse_two = norm_forward(hidden_one + branch_two, gain_two, shift_two)
    out_grad = own_rows(cotangent.reshape(row_count, width)).astype(jnp.float32)
    second_grad, gain_two_grad, shift_two_grad = norm_backward(
        out_grad, normed_two, inverse_two, gain_two
    )
    second_low = spread_rows(second_grad.astype(jnp.bfloat16))
    down_grad = jnp.einsum("rf,rd->fd", activated, second_low, preferred_element_type=jnp.float32)
    act_grad = jnp.einsum("rd,fd->rf", second_low, down_weight, preferred_element_type=jnp.float32)
    slope = (
        0.5 * (1.0 + jax.scipy.special.erf(pre_act * SQRT_HALF))
        + pre_act * jnp.exp(-0.5 * pre_act * pre_act) * INV_SQRT_TAU
    )
    pre_grad = (act_grad * slope).astype(jnp.bfloat16)
    in_grad = jnp.einsum("rd,rf->df", hidden_low, pre_grad, preferred_element_type=jnp.float32)
    hidden_grad = second_grad + reduce_heads(
        jnp.einsum("rf,df->rd", pre_grad, in_weight, preferred_element_type=jnp.float32)
    )
    first_grad, gain_one_grad, shift_one_grad = norm_backward(
        hidden_grad, normed_one, inverse_one, gain_one
    )
    first_low = spread_rows(first_grad.astype(jnp.bfloat16))
    out_weight_grad = jnp.einsum(
        "rj,rd->jd", attended_low, first_low, preferred_element_type=jnp.float32
    )
    heads_grad = jnp.einsum("rd,jd->rj", first_low, out_weight, preferred_element_type=jnp.float32)
    heads_grad = heads_grad.astype(jnp.bfloat16).reshape(seqs, piece_len, heads_here, head_size)
    row_dot = jnp.swapaxes(jnp.sum(heads_grad.astype(jnp.float32) * attended, axis=-1), 1, 2)
    back_state = (
        jnp.zeros((seqs, piece_len, heads_here, head_size), jnp.float32),
        jnp.zeros((seqs, full_len, heads_here, head_size), jnp.float32),
        jnp.zeros((seqs, full_len, heads_here, head_size), jnp.float32),
    )
    backward_key_piece = lax.all_gather(keys, "ctx", axis=1, tiled=True)
    backward_value_piece = lax.all_gather(values, "ctx", axis=1, tiled=True)
    needed, backward_doc_keys = touches()

    def backward_update(state):
        scores = masked_scores(backward_key_piece, backward_doc_keys)
        probs = jnp.exp(scores - log_total[..., None])
        value_part = jnp.einsum(
            "shqk,sqhd->skhd",
            probs.astype(jnp.bfloat16),
            heads_grad,
            preferred_element_type=jnp.float32,
        )
        prob_grad = jnp.einsum(
            "sqhd,skhd->shqk", heads_grad, backward_value_piece, preferred_element_type=jnp.float32
        )
        score_grad = (probs * (prob_grad - row_dot[..., None])).astype(jnp.bfloat16)
        query_grad = (
            jnp.einsum(
                "shqk,skhd->sqhd",
                score_grad,
                backward_key_piece,
                preferred_element_type=jnp.float32,
            )
            * scale
        )
        key_part = (
            jnp.einsum("shqk,sqhd->skhd", score_grad, queries, preferred_element_type=jnp.float32)
            * scale
        )
        return (query_grad, key_part, value_part)

    query_grad, key_grad_all, value_grad_all = lax.cond(
        needed, backward_update, lambda state: state, back_state
    )
    key_grad, value_grad = (
        lax.psum_scatter(
            key_grad_all.astype(jnp.bfloat16), "ctx", scatter_dimension=1, tiled=True
        ).astype(jnp.float32),
        lax.psum_scatter(
            value_grad_all.astype(jnp.bfloat16), "ctx", scatter_dimension=1, tiled=True
        ).astype(jnp.float32),
    )
    query_low = (
        rotate_heads(query_grad, positions, head_size, -1.0)
        .astype(jnp.bfloat16)
        .reshape(row_count, local_width)
    )
    key_low = (
        rotate_heads(key_grad, positions, head_size, -1.0)
        .astype(jnp.bfloat16)
        .reshape(row_count, local_width)
    )
    value_low = value_grad.astype(jnp.bfloat16).reshape(row_count, local_width)
    query_weight_grad = jnp.einsum(
        "rd,rj->dj", tokens, query_low, preferred_element_type=jnp.float32
    )
    key_weight_grad = jnp.einsum("rd,rj->dj", tokens, key_low, preferred_element_type=jnp.float32)
    value_weight_grad = jnp.einsum(
        "rd,rj->dj", tokens, value_low, preferred_element_type=jnp.float32
    )
    input_part = jnp.einsum(
        "rj,dj->rd", query_low, query_weight, preferred_element_type=jnp.float32
    )
    input_part = input_part + jnp.einsum(
        "rj,dj->rd", key_low, key_weight, preferred_element_type=jnp.float32
    )
    input_part = input_part + jnp.einsum(
        "rj,dj->rd", value_low, value_weight, preferred_element_type=jnp.float32
    )
    input_grad = first_grad + reduce_heads(input_part)
    norm_terms = jnp.stack([gain_one_grad, shift_one_grad, gain_two_grad, shift_two_grad])[None]
    output, input_grad, norm_terms = (
        lax.all_gather(output.astype(jnp.bfloat16), "tp", axis=0, tiled=True).astype(output.dtype),
        lax.all_gather(input_grad.astype(jnp.bfloat16), "tp", axis=0, tiled=True).astype(
            input_grad.dtype
        ),
        lax.all_gather(norm_terms.astype(jnp.bfloat16), "tp", axis=0, tiled=True).astype(
            norm_terms.dtype
        ),
    )
    norm_terms = jnp.sum(norm_terms, axis=0)
    gain_one_grad, shift_one_grad, gain_two_grad, shift_two_grad = (
        norm_terms[0],
        norm_terms[1],
        norm_terms[2],
        norm_terms[3],
    )
    shares = (
        lax.psum_scatter(
            query_weight_grad.astype(jnp.bfloat16), "dp", scatter_dimension=0, tiled=True
        ).astype(jnp.float32),
        lax.psum_scatter(
            key_weight_grad.astype(jnp.bfloat16), "dp", scatter_dimension=0, tiled=True
        ).astype(jnp.float32),
        lax.psum_scatter(
            value_weight_grad.astype(jnp.bfloat16), "dp", scatter_dimension=0, tiled=True
        ).astype(jnp.float32),
        lax.psum_scatter(
            out_weight_grad.astype(jnp.bfloat16), "dp", scatter_dimension=1, tiled=True
        ).astype(jnp.float32),
        lax.psum_scatter(
            in_grad.astype(jnp.bfloat16), "dp", scatter_dimension=0, tiled=True
        ).astype(jnp.float32),
        lax.psum_scatter(
            down_grad.astype(jnp.bfloat16), "dp", scatter_dimension=1, tiled=True
        ).astype(jnp.float32),
        lax.psum_scatter(
            gain_one_grad.astype(jnp.bfloat16), "dp", scatter_dimension=0, tiled=True
        ).astype(jnp.float32),
        lax.psum_scatter(
            shift_one_grad.astype(jnp.bfloat16), "dp", scatter_dimension=0, tiled=True
        ).astype(jnp.float32),
        lax.psum_scatter(
            gain_two_grad.astype(jnp.bfloat16), "dp", scatter_dimension=0, tiled=True
        ).astype(jnp.float32),
        lax.psum_scatter(
            shift_two_grad.astype(jnp.bfloat16), "dp", scatter_dimension=0, tiled=True
        ).astype(jnp.float32),
    )
    totals = (
        lax.psum(shares[0].astype(jnp.bfloat16), "ctx").astype(jnp.float32),
        lax.psum(shares[1].astype(jnp.bfloat16), "ctx").astype(jnp.float32),
        lax.psum(shares[2].astype(jnp.bfloat16), "ctx").astype(jnp.float32),
        lax.psum(shares[3].astype(jnp.bfloat16), "ctx").astype(jnp.float32),
        lax.psum(shares[4].astype(jnp.bfloat16), "ctx").astype(jnp.float32),
        lax.psum(shares[5].astype(jnp.bfloat16), "ctx").astype(jnp.float32),
        lax.psum(shares[6].astype(jnp.bfloat16), "ctx").astype(jnp.float32),
        lax.psum(shares[7].astype(jnp.bfloat16), "ctx").astype(jnp.float32),
        lax.psum(shares[8].astype(jnp.bfloat16), "ctx").astype(jnp.float32),
        lax.psum(shares[9].astype(jnp.bfloat16), "ctx").astype(jnp.float32),
    )
    return (
        output.reshape(seqs, piece_len, width),
        input_grad.reshape(seqs, piece_len, width),
        totals[0],
        totals[1],
        totals[2],
        totals[3],
        totals[4],
        totals[5],
        totals[6],
        totals[7],
        totals[8],
        totals[9],
    )


def solution(mesh):
    return jax.shard_map(
        body,
        mesh=mesh,
        in_specs=(
            P("dp", "ctx", None),
            P("dp", "ctx"),
            P("dp", "ctx"),
            P("dp", "tp"),
            P("dp", "tp"),
            P("dp", "tp"),
            P("tp", "dp"),
            P("dp", "tp"),
            P("tp", "dp"),
            P("dp"),
            P("dp"),
            P("dp"),
            P("dp"),
            P("dp", "ctx", None),
        ),
        out_specs=(
            P("dp", "ctx", None),
            P("dp", "ctx", None),
            P("dp", "tp"),
            P("dp", "tp"),
            P("dp", "tp"),
            P("tp", "dp"),
            P("dp", "tp"),
            P("tp", "dp"),
            P("dp"),
            P("dp"),
            P("dp"),
            P("dp"),
        ),
        check_vma=False,
    )
```

profile of v0, /device:TPU:0, one launch (start us, length us, event | category | flops | bytes accessed | tf_op | source)
XLA Modules:
  0.0 972.7 jit_solution(8596426434265717203)
XLA Ops:
  8.1 10.4 %all_gather.63 = bf16[1024,256]{1,0:T(8,128)(2,1)S(1)} all-gather(bf16[512,256]{1,0:T(8,128)(2,1)} %param.23), channel_id=1, replica_groups=mesh['dp'=2,'ctx'=4,'tp'=4] {'dp'}, dimensions={0}, use_global_device_ids=true | all-gather | bytes 786432 | tf_op jit(solution)/shard_map/all_gather | solution.py:75
  45.1 13.8 %all_gather.59 = s32[1,4096]{1,0:T(1,128)S(1)} all-gather(s32[1,1024]{1,0:T(1,128)S(1)} %copy-done.25), channel_id=1, replica_groups=mesh['dp'=2,'ctx'=4,'tp'=4] {'ctx'}, dimensions={1}, use_global_device_ids=true | all-gather | bytes 20480 | tf_op jit(solution)/shard_map/all_gather | solution.py:86
  69.8 46.2 %all-gather.15.cloned.1.call-done = bf16[1,4096,4,64]{1,3,2,0:T(8,128)(2,1)} async-done(((bf16[1,1024,4,64]{1,3,2,0:T(8,128)(2,1)}), bf16[1,4096,4,64]{1,3,2,0:T(8,128)(2,1)}) %all-gather.15.cloned.1.call-update) | async-done | bytes 2097168 | tf_op jit(solution)/shard_map/all_gather | solution.py:133
  116.0 81.0 %conditional.2 = (f32[1,4,1024]{2,1,0:T(4,128)S(1)}, f32[1,4,1024]{2,1,0:T(4,128)}, f32[1,1024,4,64]{1,3,2,0:T(8,128)S(1)}, f32[1,4,1024]{2,1,0:T(4,128)S(1)}) conditional(s32[]{:T(128)} %convert_element_type.302, () %tuple.32, (s32[1,1024]{1,0:T(1,128)S(1)}, s32[1,4096]{1,0:T(1,128)S(1)}, bf16[1,1024,4,64]{1,3,2,0:T(8,128)(2,1)S(1)}, ...), branch_computations={%region_4.0_spmd, %region_5.8_spmd} | conditional | flops 4483981312 | bytes 232476736 | solution.py:153
  120.9 25.9 %fusion = (f32[4,1024]{1,0:T(4,128)S(1)}, f32[4,1024,4096]{2,1,0:T(8,128)}) fusion(pred[1024,4096]{1,0:T(8,128)(4,1)} %broadcast_compare_fusion, bf16[1,4096,4,64]{1,3,2,0:T(8,128)(2,1)S(1)} %copy-done.2, bf16[1,1024,4,64]{1,3,2,0:T(8,128)(2,1)S(1)} %get-tuple-element.51), kind=kOutput, calls=%fused_computation.2 | convolution fusion | flops 2197811200 | bytes 73940992 | tf_op jit(solution)/shard_map/cond/branch_1_fun/sqhd,skhd->shqk/dot_general | solution.py:122
  146.8 23.3 %fusion.2 = f32[4,1024]{1,0:T(4,128)} fusion(f32[4,1024,4096]{2,1,0:T(8,128)} %get-tuple-element.155, f32[4,1024]{1,0:T(4,128)S(1)} %broadcast_maximum_fusion, pred[1024,4096]{1,0:T(8,128)(4,1)} %broadcast_compare_fusion), kind=kLoop, calls=%fused_computation.4 | loop fusion | flops 67104768 | bytes 71335936 | tf_op jit(solution)/shard_map/cond/branch_1_fun/reduce_sum | solution.py:143
  170.9 26.1 %fusion.14 = f32[1,1024,4,64]{1,3,2,0:T(8,128)S(1)} fusion(bf16[1,4096,4,64]{1,3,2,0:T(8,128)(2,1)} %get-tuple-element.53, f32[4,1024,4096]{2,1,0:T(8,128)} %get-tuple-element.155, f32[4,1024]{1,0:T(4,128)S(1)} %broadcast_maximum_fusion, pred[1024,4096]{1,0:T(8,128)(4,1)} %broadcast_compare_fusion, f32[1024,4]{0,1:T(4,128)S(1)} %get-tuple-element.144), kind=kOutput, calls=%fused_computation.12 | convolution fusion | flops 2214854656 | bytes 74481664 | tf_op jit(solution)/shard_map/cond/branch_1_fun/shqk,skhd->sqhd/dot_general | solution.py:144
  210.2 20.7 %reduce-scatter.13.cloned.1.call-done = bf16[256,1024]{1,0:T(8,128)(2,1)} async-done(((bf16[1024,1024]{1,0:T(8,128)(2,1)}), bf16[256,1024]{1,0:T(8,128)(2,1)}) %reduce-scatter.13.cloned.1.call-update) | async-done | bytes 524304 | tf_op jit(solution)/shard_map/reduce_scatter | solution.py:97
  236.8 22.2 %all-gather.17.cloned.1.call-done = bf16[1024,1024]{1,0:T(8,128)(2,1)} async-done(((bf16[256,1024]{1,0:T(8,128)(2,1)}), bf16[1024,1024]{1,0:T(8,128)(2,1)}) %all-gather.17.cloned.1.call-update) | async-done | bytes 2097168 | tf_op jit(solution)/shard_map/all_gather | solution.py:102
  259.1 14.3 %fusion.50 = (bf16[1024,1024]{1,0:T(8,128)(2,1)}, f32[1024,1024]{1,0:T(8,128)}) fusion(bf16[1024,1024]{1,0:T(8,128)(2,1)} %all-gather.17.cloned.1.call-done, bf16[1024,1024]{1,0:T(8,128)(2,1)} %all-gather.19.cloned.1.call-done), kind=kOutput, calls=%fused_computation.46 | convolution fusion | flops 2215641088 | bytes 10485760 | tf_op jit(solution)/shard_map/dot_general | solution.py:161
  273.4 20.1 %all-gather.21.cloned.1.call-done = bf16[1024,1024]{1,0:T(8,128)(2,1)} async-done(((bf16[1024,512]{1,0:T(8,128)(2,1)}), bf16[1024,1024]{1,0:T(8,128)(2,1)}) %all-gather.21.cloned.1.call-update) | async-done | bytes 2097168 | tf_op jit(solution)/shard_map/all_gather | solution.py:78
  308.3 22.5 %reduce-scatter.15.cloned.1.call-done = bf16[256,1024]{1,0:T(8,128)(2,1)} async-done(((bf16[1024,1024]{1,0:T(8,128)(2,1)}), bf16[256,1024]{1,0:T(8,128)(2,1)}) %reduce-scatter.15.cloned.1.call-update) | async-done | bytes 524304 | tf_op jit(solution)/shard_map/reduce_scatter | solution.py:97
  337.5 22.5 %all-gather.25.cloned.1.call-done = bf16[1024,1024]{1,0:T(8,128)(2,1)} async-done(((bf16[256,1024]{1,0:T(8,128)(2,1)}), bf16[1024,1024]{1,0:T(8,128)(2,1)}) %all-gather.25.cloned.1.call-update) | async-done | bytes 2097168 | tf_op jit(solution)/shard_map/all_gather | solution.py:102
  371.5 31.3 %reduce-scatter.17.cloned.1.call-done = bf16[256,1024]{1,0:T(8,128)(2,1)} async-done(((bf16[1024,1024]{1,0:T(8,128)(2,1)}), bf16[256,1024]{1,0:T(8,128)(2,1)}) %reduce-scatter.17.cloned.1.call-update) | async-done | bytes 524304 | tf_op jit(solution)/shard_map/reduce_scatter | solution.py:97
  408.0 22.7 %all-gather.27.cloned.1.call-done = bf16[1024,1024]{1,0:T(8,128)(2,1)} async-done(((bf16[256,1024]{1,0:T(8,128)(2,1)}), bf16[1024,1024]{1,0:T(8,128)(2,1)}) %all-gather.27.cloned.1.call-update) | async-done | bytes 2097168 | tf_op jit(solution)/shard_map/all_gather | solution.py:102
  434.2 129.8 %conditional.3 = (bf16[1,4096,4,64]{1,3,2,0:T(8,128)(2,1)}, bf16[1,4096,4,64]{1,3,2,0:T(8,128)(2,1)}, f32[1,1024,4,32]{1,3,2,0:T(8,128)}, f32[1,1024,4,32]{1,3,2,0:T(8,128)S(1)}) conditional(s32[]{:T(128)} %convert_element_type.302, () %tuple.34, (s32[1,1024]{1,0:T(1,128)S(1)}, s32[1,4096]{1,0:T(1,128)S(1)}, ...), branch_computations={%region_20.21_spmd, %region_21.22_spmd} | conditional | flops 10911748096 | bytes 349294720 | solution.py:228
  439.0 23.1 %fusion.34 = f32[4,1024,4096]{2,1,0:T(8,128)} fusion(bf16[1,4096,4,64]{1,3,2,0:T(8,128)(2,1)S(1)} %get-tuple-element.57, bf16[1,1024,4,64]{1,3,2,0:T(8,128)(2,1)S(1)} %get-tuple-element.56), kind=kOutput, calls=%fused_computation.31 | convolution fusion | flops 2147483648 | bytes 69730304 | tf_op jit(solution)/shard_map/cond/branch_1_fun/sqhd,skhd->shqk/dot_general | solution.py:122
  462.2 28.2 %fusion.28 = bf16[1,4096,4,64]{1,3,2,0:T(8,128)(2,1)} fusion(f32[4,1024,4096]{2,1,0:T(8,128)} %fusion.34, f32[4,1024]{1,0:T(4,128)S(1)} %add_bitcast_fusion, pred[1024,4096]{1,0:T(8,128)(4,1)} %broadcast_compare_fusion.1, bf16[1,1024,4,64]{1,3,2,0:T(8,128)(2,1)S(1)} %get-tuple-element.60), kind=kOutput, calls=%fused_computation.27 | convolution fusion | flops 2214592512 | bytes 73940992 | tf_op jit(solution)/shard_map/cond/branch_1_fun/shqk,sqhd->skhd/dot_general | solution.py:203
  490.3 41.9 %multiply_convert_fusion = bf16[4,1024,4096]{2,1,0:T(8,128)(2,1)} fusion(f32[4,1024,4096]{2,1,0:T(8,128)} %fusion.34, f32[4,1024]{1,0:T(4,128)S(1)} %bitcast.238, f32[4,1024]{1,0:T(4,128)S(1)} %add_bitcast_fusion, pred[1024,4096]{1,0:T(8,128)(4,1)} %broadcast_compare_fusion.1, bf16[1,4096,4,64]{1,3,2,0:T(8,128)(2,1)} %get-tuple-element.61, ...), kind=kOutput, calls=%fused_computation.19 | convolution fusion | flops 2248146944 | bytes 107511808 | tf_op jit(solution)/shard_map/cond/branch_1_fun/sqhd,skhd->shqk/dot_general | solution.py:209
  532.2 15.6 %fusion.39 = f32[1,1024,4,64]{1,3,2,0:T(8,128)S(1)} fusion(bf16[4,1024,4096]{2,1,0:T(8,128)(2,1)} %multiply_convert_fusion, bf16[1,4096,4,64]{1,3,2,0:T(8,128)(2,1)S(1)} %copy-done.4), kind=kOutput, calls=%fused_computation.34 | convolution fusion | flops 2147745792 | bytes 36700160 | tf_op jit(solution)/shard_map/cond/branch_1_fun/shqk,skhd->sqhd/dot_general | solution.py:214
  547.8 15.1 %fusion.27 = bf16[1,4096,4,64]{1,3,2,0:T(8,128)(2,1)} fusion(bf16[4,1024,4096]{2,1,0:T(8,128)(2,1)} %multiply_convert_fusion, bf16[1,1024,4,64]{1,3,2,0:T(8,128)(2,1)S(1)} %get-tuple-element.56), kind=kOutput, calls=%fused_computation.26 | convolution fusion | flops 2149580800 | bytes 36175872 | tf_op jit(solution)/shard_map/cond/branch_1_fun/shqk,sqhd->skhd/dot_general | solution.py:223
  580.4 27.4 %reduce-scatter.21.cloned.1.call-done = bf16[1,1024,4,64]{1,3,2,0:T(8,128)(2,1)} async-done(((bf16[1,4096,4,64]{1,3,2,0:T(8,128)(2,1)}), bf16[1,1024,4,64]{1,3,2,0:T(8,128)(2,1)}) %reduce-scatter.21.cloned.1.call-update) | async-done | bytes 524304 | tf_op jit(solution)/shard_map/reduce_scatter | solution.py:235
  610.4 43.1 %reduce-scatter.19.cloned.1.call-done = bf16[1,1024,4,64]{1,3,2,0:T(8,128)(2,1)} async-done(((bf16[1,4096,4,64]{1,3,2,0:T(8,128)(2,1)}), bf16[1,1024,4,64]{1,3,2,0:T(8,128)(2,1)}) %reduce-scatter.19.cloned.1.call-update) | async-done | bytes 524304 | tf_op jit(solution)/shard_map/reduce_scatter | solution.py:232
  667.2 20.3 %reduce-scatter.33.cloned.1.call-done = bf16[512,1024]{1,0:T(8,128)(2,1)} async-done(((bf16[1024,1024]{1,0:T(8,128)(2,1)}), bf16[512,1024]{1,0:T(8,128)(2,1)}) %reduce-scatter.33.cloned.1.call-update) | async-done | bytes 1048592 | tf_op jit(solution)/shard_map/reduce_scatter | solution.py:297
  687.5 34.2 %reduce-scatter.35.cloned.1.call-done = bf16[1024,512]{1,0:T(8,128)(2,1)} async-done(((bf16[1024,1024]{1,0:T(8,128)(2,1)}), bf16[1024,512]{1,0:T(8,128)(2,1)}) %reduce-scatter.35.cloned.1.call-update) | async-done | bytes 1048592 | tf_op jit(solution)/shard_map/reduce_scatter | solution.py:300
  721.7 16.8 %reduce-scatter.31.cloned.1.call-done = bf16[256,512]{1,0:T(8,128)(2,1)} async-done(((bf16[256,1024]{1,0:T(8,128)(2,1)}), bf16[256,512]{1,0:T(8,128)(2,1)}) %reduce-scatter.31.cloned.1.call-update) | async-done | bytes 262160 | tf_op jit(solution)/shard_map/reduce_scatter | solution.py:294
  738.5 17.5 %reduce-scatter.29.cloned.1.call-done = bf16[512,256]{0,1:T(8,128)(2,1)} async-done(((bf16[1024,256]{0,1:T(8,128)(2,1)}), bf16[512,256]{0,1:T(8,128)(2,1)}) %reduce-scatter.29.cloned.1.call-update) | async-done | bytes 262160 | tf_op jit(solution)/shard_map/reduce_scatter | solution.py:291
  756.0 17.3 %reduce-scatter.27.cloned.1.call-done = bf16[512,256]{0,1:T(8,128)(2,1)} async-done(((bf16[1024,256]{0,1:T(8,128)(2,1)}), bf16[512,256]{0,1:T(8,128)(2,1)}) %reduce-scatter.27.cloned.1.call-update) | async-done | bytes 262160 | tf_op jit(solution)/shard_map/reduce_scatter | solution.py:288
  773.3 17.5 %reduce-scatter.25.cloned.1.call-done = bf16[512,256]{0,1:T(8,128)(2,1)} async-done(((bf16[1024,256]{0,1:T(8,128)(2,1)}), bf16[512,256]{0,1:T(8,128)(2,1)}) %reduce-scatter.25.cloned.1.call-update) | async-done | bytes 262160 | tf_op jit(solution)/shard_map/reduce_scatter | solution.py:285
  790.9 34.1 %reduce-scatter.23.cloned.1.call-done = bf16[256,1024]{1,0:T(8,128)(2,1)} async-done(((bf16[1024,1024]{1,0:T(8,128)(2,1)}), bf16[256,1024]{1,0:T(8,128)(2,1)}) %reduce-scatter.23.cloned.1.call-update) | async-done | bytes 524304 | tf_op jit(solution)/shard_map/reduce_scatter | solution.py:97
  844.6 12.0 %all-reduce.4 = (bf16[512]{0:T(512)(128)(2,1)S(1)}, bf16[512]{0:T(512)(128)(2,1)S(1)}, bf16[512]{0:T(512)(128)(2,1)S(1)}, bf16[512]{0:T(512)(128)(2,1)S(1)}) all-reduce(bf16[512]{0:T(512)(128)(2,1)S(1)} %dynamic-slice.3, bf16[512]{0:T(512)(128)(2,1)S(1)} %dynamic-slice.5, ...), channel_id=1, replica_groups=mesh['dp'=2,'ctx'=4,'tp'=4] {'ctx'}, use_global_device_ids=true, to_apply=%region_43.44 | all-reduce | flops 2048 | bytes 8192 | tf_op jit(solution)/shard_map/psum | solution.py:323
  859.0 90.2 %all-reduce.9.cloned.1.call-done = (bf16[512,256]{0,1:T(8,128)(2,1)}, bf16[512,256]{0,1:T(8,128)(2,1)}, bf16[512,256]{0,1:T(8,128)(2,1)}, bf16[256,512]{1,0:T(8,...) async-done(((bf16[512,256]{0,1:T(8,128)(2,1)}, bf16[512,256]{0,1:T(8,128)(2,1)}, bf16[512,256]{0,1:T(8,128)(2,1)}, bf16[256,512]{1,0:T(8,128)(2,1)}, ...) | async-done | bytes 3145744 | tf_op jit(solution)/shard_map/psum | solution.py:317
  (224 shorter events, 176.3 us)
Async XLA Ops:
  8.0 61.8 %all-gather.31.cloned.1.call-start = ((), (), s32[]{:S(2)}) async-start(), calls=%async_computation.32 | async-start | bytes 2621440 | tf_op jit(solution)/shard_map/all_gather | solution.py:134
  21.9 94.1 %all-gather.15.cloned.1.call-start = ((), (), s32[]{:S(2)}) async-start(), calls=%async_computation.12 | async-start | bytes 2621440 | tf_op jit(solution)/shard_map/all_gather | solution.py:133
  45.0 185.9 %reduce-scatter.13.cloned.1.call-start = ((), (), s32[]{:S(2)}) async-start(), calls=%async_computation.13 | async-start | bytes 2621440 | tf_op jit(solution)/shard_map/reduce_scatter | solution.py:97
  69.8 128.1 %copy-start.15 = (bf16[256,1024]{1,0:T(8,128)(2,1)}, bf16[256,1024]{1,0:T(8,128)(2,1)S(1)}, u32[]{:S(2)}) copy-start(bf16[256,1024]{1,0:T(8,128)(2,1)S(1)} %all_gather.65) | copy-start | bytes 1572868
  200.8 36.0 %all-gather.19.cloned.1.call-start = ((), (), s32[]{:S(2)}) async-start(), calls=%async_computation.15 | async-start | bytes 3145728 | tf_op jit(solution)/shard_map/all_gather | solution.py:77
  201.4 57.7 %all-gather.17.cloned.1.call-start = ((), (), s32[]{:S(2)}) async-start(), calls=%async_computation.14 | async-start | bytes 2621440 | tf_op jit(solution)/shard_map/all_gather | solution.py:102
  236.1 57.3 %all-gather.21.cloned.1.call-start = ((), (), s32[]{:S(2)}) async-start(), calls=%async_computation.16 | async-start | bytes 3145728 | tf_op jit(solution)/shard_map/all_gather | solution.py:78
  236.7 94.0 %reduce-scatter.15.cloned.1.call-start = ((), (), s32[]{:S(2)}) async-start(), calls=%async_computation.17 | async-start | bytes 2621440 | tf_op jit(solution)/shard_map/reduce_scatter | solution.py:97
  293.5 37.3 %copy-start = (bf16[256,1024]{1,0:T(8,128)(2,1)S(1)}, bf16[256,1024]{1,0:T(8,128)(2,1)}, u32[]{:S(2)}) copy-start(bf16[256,1024]{1,0:T(8,128)(2,1)} %reduce-scatter.13.cloned.1.call-done) | copy-start | bytes 1572868
  299.4 60.6 %all-gather.25.cloned.1.call-start = ((), (), s32[]{:S(2)}) async-start(), calls=%async_computation.19 | async-start | bytes 2621440 | tf_op jit(solution)/shard_map/all_gather | solution.py:102
  337.3 65.5 %reduce-scatter.17.cloned.1.call-start = ((), (), s32[]{:S(2)}) async-start(), calls=%async_computation.20 | async-start | bytes 2621440 | tf_op jit(solution)/shard_map/reduce_scatter | solution.py:97
  371.5 59.3 %all-gather.27.cloned.1.call-start = ((), (), s32[]{:S(2)}) async-start(), calls=%async_computation.21 | async-start | bytes 2621440 | tf_op jit(solution)/shard_map/all_gather | solution.py:102
  408.0 199.8 %reduce-scatter.21.cloned.1.call-start = ((), (), s32[]{:S(2)}) async-start(), calls=%async_computation.23 | async-start | bytes 2621440 | tf_op jit(solution)/shard_map/reduce_scatter | solution.py:235
  434.3 27.9 %copy-start.20 = (bf16[1,1024,4,64]{1,3,2,0:T(8,128)(2,1)}, bf16[1,1024,4,64]{1,3,2,0:T(8,128)(2,1)S(1)}, u32[]{:S(2)}) copy-start(bf16[1,1024,4,64]{1,3,2,0:T(8,128)(2,1)S(1)} %get-tuple-element.60) | copy-start | bytes 1572868 | tf_op jit(solution)/shard_map/cond
  490.3 41.9 %copy-start.4 = (bf16[1,4096,4,64]{1,3,2,0:T(8,128)(2,1)S(1)}, bf16[1,4096,4,64]{1,3,2,0:T(8,128)(2,1)}, u32[]{:S(2)}) copy-start(bf16[1,4096,4,64]{1,3,2,0:T(8,128)(2,1)} %copy-done.3) | copy-start | bytes 6291460 | tf_op jit(solution)/shard_map/cond
  564.0 89.5 %reduce-scatter.19.cloned.1.call-start = ((), (), s32[]{:S(2)}) async-start(), calls=%async_computation.22 | async-start | bytes 2621440 | tf_op jit(solution)/shard_map/reduce_scatter | solution.py:232
  564.8 122.7 %reduce-scatter.33.cloned.1.call-start = ((), (), s32[]{:S(2)}) async-start(), calls=%async_computation.30 | async-start | bytes 3145728 | tf_op jit(solution)/shard_map/reduce_scatter | solution.py:297
  570.9 150.8 %reduce-scatter.35.cloned.1.call-start = ((), (), s32[]{:S(2)}) async-start(), calls=%async_computation.31 | async-start | bytes 3145728 | tf_op jit(solution)/shard_map/reduce_scatter | solution.py:300
  577.0 30.9 %copy-start.11 = (bf16[1,1024,1024]{2,1,0:T(8,128)(2,1)S(1)}, bf16[1,1024,1024]{2,1,0:T(8,128)(2,1)}, u32[]{:S(2)}) copy-start(bf16[1,1024,1024]{2,1,0:T(8,128)(2,1)} %param.18) | copy-start | bytes 6291460
  577.0 77.7 %copy-start.17 = (f32[1024,32]{0,1:T(8,128)S(1)}, f32[1024,32]{0,1:T(8,128)}, u32[]{:S(2)}) copy-start(f32[1024,32]{0,1:T(8,128)} %copy-done.16) | copy-start | bytes 393220
  577.0 77.7 %copy-start.21 = (f32[1024,32]{0,1:T(8,128)S(1)}, f32[1024,32]{0,1:T(8,128)}, u32[]{:S(2)}) copy-start(f32[1024,32]{0,1:T(8,128)} %get-tuple-element.169) | copy-start | bytes 393220
  577.0 161.5 %reduce-scatter.31.cloned.1.call-start = ((), (), s32[]{:S(2)}) async-start(), calls=%async_computation.29 | async-start | bytes 786432 | tf_op jit(solution)/shard_map/reduce_scatter | solution.py:294
  580.3 175.6 %reduce-scatter.29.cloned.1.call-start = ((), (), s32[]{:S(2)}) async-start(), calls=%async_computation.28 | async-start | bytes 786432 | tf_op jit(solution)/shard_map/reduce_scatter | solution.py:291
  610.4 162.9 %reduce-scatter.27.cloned.1.call-start = ((), (), s32[]{:S(2)}) async-start(), calls=%async_computation.27 | async-start | bytes 786432 | tf_op jit(solution)/shard_map/reduce_scatter | solution.py:288
  659.3 131.5 %reduce-scatter.25.cloned.1.call-start = ((), (), s32[]{:S(2)}) async-start(), calls=%async_computation.26 | async-start | bytes 786432 | tf_op jit(solution)/shard_map/reduce_scatter | solution.py:285
  662.6 162.3 %reduce-scatter.23.cloned.1.call-start = ((), (), s32[]{:S(2)}) async-start(), calls=%async_computation.24 | async-start | bytes 2621440 | tf_op jit(solution)/shard_map/reduce_scatter | solution.py:97
  666.4 158.6 %copy-start.12 = (f32[256,1024]{1,0:T(8,128)S(1)}, f32[256,1024]{1,0:T(8,128)}, u32[]{:S(2)}) copy-start(f32[256,1024]{1,0:T(8,128)} %get-tuple-element.147) | copy-start | bytes 3145732
  666.4 161.8 %copy-start.36 = (u32[32]{0:T(128)S(1)}, u32[32]{0:T(128)}, u32[]{:S(2)}) copy-start(u32[32]{0:T(128)} %constant.140) | copy-start | bytes 388
  666.4 163.0 %copy-start.26 = (bf16[1024]{0:T(1024)(128)(2,1)S(1)}, bf16[1024]{0:T(1024)(128)(2,1)}, u32[]{:S(2)}) copy-start(bf16[1024]{0:T(1024)(128)(2,1)} %get-tuple-element.117) | copy-start | bytes 6148
  666.4 163.1 %all-gather.23.cloned.1.call-start = ((), (), s32[]{:S(2)}) async-start(), calls=%async_computation.18 | async-start | bytes 2621440 | tf_op jit(solution)/shard_map/all_gather | solution.py:269
  667.1 282.0 %all-reduce.9.cloned.1.call-start = ((), (), s32[]{:S(2)}) async-start(), calls=%async_computation.33 | async-start | bytes 6291456 | tf_op jit(solution)/shard_map/psum | solution.py:317
  790.8 170.3 %all-gather.29.cloned.1.call-start = ((), (), s32[]{:S(2)}) async-start(), calls=%async_computation.25 | async-start | bytes 2621440 | tf_op jit(solution)/shard_map/all_gather | solution.py:270
  (28 other events, 197.0 us)
Sparse Core Ops, SparseCore 0:
  22.0 47.3 all-gather.30
  71.5 44.4 all-gather.14
  200.9 29.9 reduce-scatter.12
  337.4 22.5 all-gather.24
  408.1 22.5 all-gather.26
  564.1 43.6 reduce-scatter.20
  610.7 42.8 reduce-scatter.18
  656.4 31.0 reduce-scatter.32
  689.8 31.8 reduce-scatter.34
  723.8 14.6 reduce-scatter.30
  741.3 14.6 reduce-scatter.28
  758.6 14.6 reduce-scatter.26
  776.1 14.6 reduce-scatter.24
  793.8 31.1 reduce-scatter.22
  827.7 121.4 all-reduce.8
Sparse Core Ops, SparseCore 1:
  202.8 31.7 all-gather.18
  236.6 22.4 all-gather.16
  260.5 32.9 all-gather.20
  299.5 31.2 reduce-scatter.14
  371.5 31.2 reduce-scatter.16
  669.3 21.6 all-gather.22
  827.1 22.5 all-gather.28
where the time goes:
time: 978 us; the launch traced here: 973 us
  waiting for transfers between devices  529 us (54%)
  matrix products  246 us (25%)
  blocking collectives  86.4 us (9%)
  other arithmetic  78 us (8%)
  between operations  19.7 us (2%)
  local copies, waits for them, and re-layouts  12 us (1%)
    reduce_scatter x4, waiting for transfers between devices, reduce_heads(): lax.psum_scatter(partial_sum.astype(jnp.bfloat16), 'tp', scatter_dimensio...  109 us
    psum x1, waiting for transfers between devices, body(): lax.psum(shares[0].astype(jnp.bfloat16), 'ctx').astype(jnp.float32)  90.2 us
    all_gather x3, waiting for transfers between devices, spread_rows(): return lax.all_gather(rows_low, 'tp', axis=0, tiled=True)  67.4 us
    dot_general x2, matrix products, masked_scores(): jnp.einsum('sqhd,skhd->shqk', queries, key_piece, preferred_element_type=...  49 us
    all_gather x1, waiting for transfers between devices, body(): key_piece = lax.all_gather(keys, 'ctx', axis=1, tiled=True)  46.2 us
    reduce_scatter x1, waiting for transfers between devices, body(): lax.psum_scatter(key_grad_all.astype(jnp.bfloat16), 'ctx', scatter_dimens...  43.1 us
    dot_general x1, matrix products, backward_update(): jnp.einsum('sqhd,skhd->shqk', heads_grad, backward_value_piece, preferred...  41.9 us
    reduce_scatter x1, waiting for transfers between devices, body(): lax.psum_scatter(down_grad.astype(jnp.bfloat16), 'dp', scatter_dimension=...  34.2 us
  transfers between devices with their start and end apart: 22, of which 18 were waited for; matrix products, arithmetic and copies ran while one was open for 8% of the time, Pallas kernels for 0%

commit v1 on v0

--- a/solution.py
+++ b/solution.py
@@ -314,7 +314,9 @@
         ).astype(jnp.float32),
     )
     totals = (
-        lax.psum(shares[0].astype(jnp.bfloat16), "ctx").astype(jnp.float32),
+        jnp.sum(lax.all_gather(shares[0].astype(jnp.bfloat16), axis_name="ctx"), axis=0).astype(
+            jnp.float32
+        ),
         lax.psum(shares[1].astype(jnp.bfloat16), "ctx").astype(jnp.float32),
         lax.psum(shares[2].astype(jnp.bfloat16), "ctx").astype(jnp.float32),
         lax.psum(shares[3].astype(jnp.bfloat16), "ctx").astype(jnp.float32),

time: 978 us -> 944 us (0.965)
  waiting for transfers between devices: 529 us -> 494 us
    psum x1, waiting for transfers between devices: 90.2 us -> 40.9 us  [body(): lax.psum(shares[1].astype(jnp.bfloat16), 'ctx').astype(jnp.float32)]
    reduce_scatter x1, waiting for transfers between devices: 20.3 us -> 34.7 us  [body(): lax.psum_scatter(in_grad.astype(jnp.bfloat16), 'dp', scatter_dimension=0,...]
    all_gather x1, waiting for transfers between devices: 0.01 us -> 13.3 us  [body(): lax.all_gather(input_grad.astype(jnp.bfloat16), 'tp', axis=0, tiled=True)]
    reduce_scatter x1, waiting for transfers between devices: 17.5 us -> 5.5 us  [body(): lax.psum_scatter(query_weight_grad.astype(jnp.bfloat16), 'dp', scatter_di...]
  transfers between devices with their start and end apart: 22 -> 23, of which waited for: 18 -> 19; matrix products, arithmetic and copies ran while one was open for 8% -> 9% of each run, Pallas kernels for 0% -> 0%
where the time goes in v1:
time: 944 us; the launch traced here: 939 us
  waiting for transfers between devices  494 us (52%)
  matrix products  245 us (26%)
  blocking collectives  86.2 us (9%)
  other arithmetic  79.8 us (8%)
  between operations  19.8 us (2%)
  local copies, waits for them, and re-layouts  12.1 us (1%)
    reduce_scatter x4, waiting for transfers between devices, reduce_heads(): lax.psum_scatter(partial_sum.astype(jnp.bfloat16), 'tp', scatter_dimensio...  108 us
    all_gather x3, waiting for transfers between devices, spread_rows(): return lax.all_gather(rows_low, 'tp', axis=0, tiled=True)  67.4 us
    dot_general x2, matrix products, masked_scores(): jnp.einsum('sqhd,skhd->shqk', queries, key_piece, preferred_element_type=...  49 us
    all_gather x1, waiting for transfers between devices, body(): key_piece = lax.all_gather(keys, 'ctx', axis=1, tiled=True)  46.1 us
    reduce_scatter x1, waiting for transfers between devices, body(): lax.psum_scatter(key_grad_all.astype(jnp.bfloat16), 'ctx', scatter_dimens...  43 us
    dot_general x1, matrix products, backward_update(): jnp.einsum('sqhd,skhd->shqk', heads_grad, backward_value_piece, preferred...  41.9 us
    psum x1, waiting for transfers between devices, body(): lax.psum(shares[1].astype(jnp.bfloat16), 'ctx').astype(jnp.float32)  40.9 us
    reduce_scatter x1, waiting for transfers between devices, body(): lax.psum_scatter(in_grad.astype(jnp.bfloat16), 'dp', scatter_dimension=0,...  34.7 us
  transfers between devices with their start and end apart: 23, of which 19 were waited for; matrix products, arithmetic and copies ran while one was open for 9% of the time, Pallas kernels for 0%

profile of v1, /device:TPU:0, one launch (start us, length us, event | category | flops | bytes accessed | tf_op | source)
XLA Modules:
  0.0 939.3 jit_solution(18179581941446967045)
XLA Ops:
  8.1 10.4 %all_gather.69 = bf16[1024,256]{1,0:T(8,128)(2,1)S(1)} all-gather(bf16[512,256]{1,0:T(8,128)(2,1)} %param.23), channel_id=1, replica_groups=mesh['dp'=2,'ctx'=4,'tp'=4] {'dp'}, dimensions={0}, use_global_device_ids=true | all-gather | bytes 786432 | tf_op jit(solution)/shard_map/all_gather | solution.py:75
  45.1 13.8 %all_gather.65 = s32[1,4096]{1,0:T(1,128)S(1)} all-gather(s32[1,1024]{1,0:T(1,128)S(1)} %copy-done.26), channel_id=1, replica_groups=mesh['dp'=2,'ctx'=4,'tp'=4] {'ctx'}, dimensions={1}, use_global_device_ids=true | all-gather | bytes 20480 | tf_op jit(solution)/shard_map/all_gather | solution.py:86
  69.8 46.1 %all-gather.17.cloned.1.call-done = bf16[1,4096,4,64]{1,3,2,0:T(8,128)(2,1)} async-done(((bf16[1,1024,4,64]{1,3,2,0:T(8,128)(2,1)}), bf16[1,4096,4,64]{1,3,2,0:T(8,128)(2,1)}) %all-gather.17.cloned.1.call-update) | async-done | bytes 2097168 | tf_op jit(solution)/shard_map/all_gather | solution.py:133
  116.0 81.1 %conditional.2 = (f32[1,4,1024]{2,1,0:T(4,128)S(1)}, f32[1,4,1024]{2,1,0:T(4,128)}, f32[1,1024,4,64]{1,3,2,0:T(8,128)S(1)}, f32[1,4,1024]{2,1,0:T(4,128)S(1)}) conditional(s32[]{:T(128)} %convert_element_type.304, () %tuple.32, (s32[1,1024]{1,0:T(1,128)S(1)}, s32[1,4096]{1,0:T(1,128)S(1)}, bf16[1,1024,4,64]{1,3,2,0:T(8,128)(2,1)S(1)}, ...), branch_computations={%region_4.0_spmd, %region_5.8_spmd} | conditional | flops 4483981312 | bytes 232476736 | solution.py:153
  121.0 25.9 %fusion = (f32[4,1024]{1,0:T(4,128)S(1)}, f32[4,1024,4096]{2,1,0:T(8,128)}) fusion(pred[1024,4096]{1,0:T(8,128)(4,1)} %broadcast_compare_fusion, bf16[1,4096,4,64]{1,3,2,0:T(8,128)(2,1)S(1)} %copy-done.2, bf16[1,1024,4,64]{1,3,2,0:T(8,128)(2,1)S(1)} %get-tuple-element.51), kind=kOutput, calls=%fused_computation.2 | convolution fusion | flops 2197811200 | bytes 73940992 | tf_op jit(solution)/shard_map/cond/branch_1_fun/sqhd,skhd->shqk/dot_general | solution.py:122
  146.9 23.3 %fusion.2 = f32[4,1024]{1,0:T(4,128)} fusion(f32[4,1024,4096]{2,1,0:T(8,128)} %get-tuple-element.154, f32[4,1024]{1,0:T(4,128)S(1)} %broadcast_maximum_fusion, pred[1024,4096]{1,0:T(8,128)(4,1)} %broadcast_compare_fusion), kind=kLoop, calls=%fused_computation.4 | loop fusion | flops 67104768 | bytes 71335936 | tf_op jit(solution)/shard_map/cond/branch_1_fun/reduce_sum | solution.py:143
  171.0 26.1 %fusion.14 = f32[1,1024,4,64]{1,3,2,0:T(8,128)S(1)} fusion(bf16[1,4096,4,64]{1,3,2,0:T(8,128)(2,1)} %get-tuple-element.53, f32[4,1024,4096]{2,1,0:T(8,128)} %get-tuple-element.154, f32[4,1024]{1,0:T(4,128)S(1)} %broadcast_maximum_fusion, pred[1024,4096]{1,0:T(8,128)(4,1)} %broadcast_compare_fusion, f32[1024,4]{0,1:T(4,128)S(1)} %get-tuple-element.143), kind=kOutput, calls=%fused_computation.12 | convolution fusion | flops 2214854656 | bytes 74481664 | tf_op jit(solution)/shard_map/cond/branch_1_fun/shqk,skhd->sqhd/dot_general | solution.py:144
  210.4 20.6 %reduce-scatter.13.cloned.1.call-done = bf16[256,1024]{1,0:T(8,128)(2,1)} async-done(((bf16[1024,1024]{1,0:T(8,128)(2,1)}), bf16[256,1024]{1,0:T(8,128)(2,1)}) %reduce-scatter.13.cloned.1.call-update) | async-done | bytes 524304 | tf_op jit(solution)/shard_map/reduce_scatter | solution.py:97
  236.9 22.2 %all-gather.19.cloned.1.call-done = bf16[1024,1024]{1,0:T(8,128)(2,1)} async-done(((bf16[256,1024]{1,0:T(8,128)(2,1)}), bf16[1024,1024]{1,0:T(8,128)(2,1)}) %all-gather.19.cloned.1.call-update) | async-done | bytes 2097168 | tf_op jit(solution)/shard_map/all_gather | solution.py:102
  259.1 14.3 %fusion.50 = (bf16[1024,1024]{1,0:T(8,128)(2,1)}, f32[1024,1024]{1,0:T(8,128)}) fusion(bf16[1024,1024]{1,0:T(8,128)(2,1)} %all-gather.19.cloned.1.call-done, bf16[1024,1024]{1,0:T(8,128)(2,1)} %all-gather.21.cloned.1.call-done), kind=kOutput, calls=%fused_computation.46 | convolution fusion | flops 2215641088 | bytes 10485760 | tf_op jit(solution)/shard_map/dot_general | solution.py:161
  273.4 20.1 %all-gather.23.cloned.1.call-done = bf16[1024,1024]{1,0:T(8,128)(2,1)} async-done(((bf16[1024,512]{1,0:T(8,128)(2,1)}), bf16[1024,1024]{1,0:T(8,128)(2,1)}) %all-gather.23.cloned.1.call-update) | async-done | bytes 2097168 | tf_op jit(solution)/shard_map/all_gather | solution.py:78
  308.3 22.5 %reduce-scatter.15.cloned.1.call-done = bf16[256,1024]{1,0:T(8,128)(2,1)} async-done(((bf16[1024,1024]{1,0:T(8,128)(2,1)}), bf16[256,1024]{1,0:T(8,128)(2,1)}) %reduce-scatter.15.cloned.1.call-update) | async-done | bytes 524304 | tf_op jit(solution)/shard_map/reduce_scatter | solution.py:97
  337.6 22.5 %all-gather.27.cloned.1.call-done = bf16[1024,1024]{1,0:T(8,128)(2,1)} async-done(((bf16[256,1024]{1,0:T(8,128)(2,1)}), bf16[1024,1024]{1,0:T(8,128)(2,1)}) %all-gather.27.cloned.1.call-update) | async-done | bytes 2097168 | tf_op jit(solution)/shard_map/all_gather | solution.py:102
  371.6 31.3 %reduce-scatter.17.cloned.1.call-done = bf16[256,1024]{1,0:T(8,128)(2,1)} async-done(((bf16[1024,1024]{1,0:T(8,128)(2,1)}), bf16[256,1024]{1,0:T(8,128)(2,1)}) %reduce-scatter.17.cloned.1.call-update) | async-done | bytes 524304 | tf_op jit(solution)/shard_map/reduce_scatter | solution.py:97
  408.1 22.7 %all-gather.29.cloned.1.call-done = bf16[1024,1024]{1,0:T(8,128)(2,1)} async-done(((bf16[256,1024]{1,0:T(8,128)(2,1)}), bf16[1024,1024]{1,0:T(8,128)(2,1)}) %all-gather.29.cloned.1.call-update) | async-done | bytes 2097168 | tf_op jit(solution)/shard_map/all_gather | solution.py:102
  434.3 130.0 %conditional.3 = (bf16[1,4096,4,64]{1,3,2,0:T(8,128)(2,1)}, bf16[1,4096,4,64]{1,3,2,0:T(8,128)(2,1)}, f32[1,1024,4,32]{1,3,2,0:T(8,128)}, f32[1,1024,4,32]{1,3,2,0:T(8,128)S(1)}) conditional(s32[]{:T(128)} %convert_element_type.304, () %tuple.34, (s32[1,1024]{1,0:T(1,128)S(1)}, s32[1,4096]{1,0:T(1,128)S(1)}, ...), branch_computations={%region_20.21_spmd, %region_21.22_spmd} | conditional | flops 10911748096 | bytes 349294720 | solution.py:228
  439.1 23.1 %fusion.34 = f32[4,1024,4096]{2,1,0:T(8,128)} fusion(bf16[1,4096,4,64]{1,3,2,0:T(8,128)(2,1)S(1)} %get-tuple-element.57, bf16[1,1024,4,64]{1,3,2,0:T(8,128)(2,1)S(1)} %get-tuple-element.56), kind=kOutput, calls=%fused_computation.31 | convolution fusion | flops 2147483648 | bytes 69730304 | tf_op jit(solution)/shard_map/cond/branch_1_fun/sqhd,skhd->shqk/dot_general | solution.py:122
  462.2 28.2 %fusion.28 = bf16[1,4096,4,64]{1,3,2,0:T(8,128)(2,1)} fusion(f32[4,1024,4096]{2,1,0:T(8,128)} %fusion.34, f32[4,1024]{1,0:T(4,128)S(1)} %add_bitcast_fusion, pred[1024,4096]{1,0:T(8,128)(4,1)} %broadcast_compare_fusion.1, bf16[1,1024,4,64]{1,3,2,0:T(8,128)(2,1)S(1)} %get-tuple-element.60), kind=kOutput, calls=%fused_computation.27 | convolution fusion | flops 2214592512 | bytes 73940992 | tf_op jit(solution)/shard_map/cond/branch_1_fun/shqk,sqhd->skhd/dot_general | solution.py:203
  490.4 41.9 %multiply_convert_fusion = bf16[4,1024,4096]{2,1,0:T(8,128)(2,1)} fusion(f32[4,1024,4096]{2,1,0:T(8,128)} %fusion.34, f32[4,1024]{1,0:T(4,128)S(1)} %bitcast.240, f32[4,1024]{1,0:T(4,128)S(1)} %add_bitcast_fusion, pred[1024,4096]{1,0:T(8,128)(4,1)} %broadcast_compare_fusion.1, bf16[1,4096,4,64]{1,3,2,0:T(8,128)(2,1)} %get-tuple-element.61, ...), kind=kOutput, calls=%fused_computation.19 | convolution fusion | flops 2248146944 | bytes 107511808 | tf_op jit(solution)/shard_map/cond/branch_1_fun/sqhd,skhd->shqk/dot_general | solution.py:209
  532.3 15.6 %fusion.39 = f32[1,1024,4,64]{1,3,2,0:T(8,128)S(1)} fusion(bf16[4,1024,4096]{2,1,0:T(8,128)(2,1)} %multiply_convert_fusion, bf16[1,4096,4,64]{1,3,2,0:T(8,128)(2,1)S(1)} %copy-done.4), kind=kOutput, calls=%fused_computation.34 | convolution fusion | flops 2147745792 | bytes 36700160 | tf_op jit(solution)/shard_map/cond/branch_1_fun/shqk,skhd->sqhd/dot_general | solution.py:214
  547.9 15.1 %fusion.27 = bf16[1,4096,4,64]{1,3,2,0:T(8,128)(2,1)} fusion(bf16[4,1024,4096]{2,1,0:T(8,128)(2,1)} %multiply_convert_fusion, bf16[1,1024,4,64]{1,3,2,0:T(8,128)(2,1)S(1)} %get-tuple-element.56), kind=kOutput, calls=%fused_computation.26 | convolution fusion | flops 2149580800 | bytes 36175872 | tf_op jit(solution)/shard_map/cond/branch_1_fun/shqk,sqhd->skhd/dot_general | solution.py:223
  565.1 43.0 %reduce-scatter.19.cloned.1.call-done = bf16[1,1024,4,64]{1,3,2,0:T(8,128)(2,1)} async-done(((bf16[1,4096,4,64]{1,3,2,0:T(8,128)(2,1)}), bf16[1,1024,4,64]{1,3,2,0:T(8,128)(2,1)}) %reduce-scatter.19.cloned.1.call-update) | async-done | bytes 524304 | tf_op jit(solution)/shard_map/reduce_scatter | solution.py:232
  628.3 25.6 %reduce-scatter.21.cloned.1.call-done = bf16[1,1024,4,64]{1,3,2,0:T(8,128)(2,1)} async-done(((bf16[1,4096,4,64]{1,3,2,0:T(8,128)(2,1)}), bf16[1,1024,4,64]{1,3,2,0:T(8,128)(2,1)}) %reduce-scatter.21.cloned.1.call-update) | async-done | bytes 524304 | tf_op jit(solution)/shard_map/reduce_scatter | solution.py:235
  670.6 34.7 %reduce-scatter.33.cloned.1.call-done = bf16[512,1024]{1,0:T(8,128)(2,1)} async-done(((bf16[1024,1024]{1,0:T(8,128)(2,1)}), bf16[512,1024]{1,0:T(8,128)(2,1)}) %reduce-scatter.33.cloned.1.call-update) | async-done | bytes 1048592 | tf_op jit(solution)/shard_map/reduce_scatter | solution.py:297
  705.3 34.6 %reduce-scatter.35.cloned.1.call-done = bf16[1024,512]{1,0:T(8,128)(2,1)} async-done(((bf16[1024,1024]{1,0:T(8,128)(2,1)}), bf16[1024,512]{1,0:T(8,128)(2,1)}) %reduce-scatter.35.cloned.1.call-update) | async-done | bytes 1048592 | tf_op jit(solution)/shard_map/reduce_scatter | solution.py:300
  739.9 16.9 %reduce-scatter.31.cloned.1.call-done = bf16[256,512]{1,0:T(8,128)(2,1)} async-done(((bf16[256,1024]{1,0:T(8,128)(2,1)}), bf16[256,512]{1,0:T(8,128)(2,1)}) %reduce-scatter.31.cloned.1.call-update) | async-done | bytes 262160 | tf_op jit(solution)/shard_map/reduce_scatter | solution.py:294
  756.8 17.3 %reduce-scatter.29.cloned.1.call-done = bf16[512,256]{0,1:T(8,128)(2,1)} async-done(((bf16[1024,256]{0,1:T(8,128)(2,1)}), bf16[512,256]{0,1:T(8,128)(2,1)}) %reduce-scatter.29.cloned.1.call-update) | async-done | bytes 262160 | tf_op jit(solution)/shard_map/reduce_scatter | solution.py:291
  774.1 17.5 %reduce-scatter.27.cloned.1.call-done = bf16[512,256]{0,1:T(8,128)(2,1)} async-done(((bf16[1024,256]{0,1:T(8,128)(2,1)}), bf16[512,256]{0,1:T(8,128)(2,1)}) %reduce-scatter.27.cloned.1.call-update) | async-done | bytes 262160 | tf_op jit(solution)/shard_map/reduce_scatter | solution.py:288
  791.7 34.1 %reduce-scatter.23.cloned.1.call-done = bf16[256,1024]{1,0:T(8,128)(2,1)} async-done(((bf16[1024,1024]{1,0:T(8,128)(2,1)}), bf16[256,1024]{1,0:T(8,128)(2,1)}) %reduce-scatter.23.cloned.1.call-update) | async-done | bytes 524304 | tf_op jit(solution)/shard_map/reduce_scatter | solution.py:97
  845.0 11.9 %all-reduce.4 = (bf16[512]{0:T(512)(128)(2,1)S(1)}, bf16[512]{0:T(512)(128)(2,1)S(1)}, bf16[512]{0:T(512)(128)(2,1)S(1)}, bf16[512]{0:T(512)(128)(2,1)S(1)}) all-reduce(bf16[512]{0:T(512)(128)(2,1)S(1)} %dynamic-slice.3, bf16[512]{0:T(512)(128)(2,1)S(1)} %dynamic-slice.5, ...), channel_id=1, replica_groups=mesh['dp'=2,'ctx'=4,'tp'=4] {'ctx'}, use_global_device_ids=true, to_apply=%region_43.44 | all-reduce | flops 2048 | bytes 8192 | tf_op jit(solution)/shard_map/psum | solution.py:325
  863.4 40.9 %all-reduce.9.cloned.1.call-done = (bf16[512,256]{0,1:T(8,128)(2,1)}, bf16[512,256]{0,1:T(8,128)(2,1)}, bf16[256,512]{1,0:T(8,128)(2,1)}, bf16[512,1024]{1,0:T(8,128)(2,1)}, bf16[1024,512]{1,0:T(8,128)(2,1)}) async-done(((bf16[512,256]{0,1:T(8,128)(2,1)}, bf16[512,256]{0,1:T(8,128)(2,1)}, bf16[256,512]{1,0:T(8,128)(2,1)}, bf16[512,1024]{1,0:T(8,128)(2,1)}, bf16[1024,512]{1,0:T(8,128)(2,1)}), ...) | async-done | bytes 2883600 | tf_op jit(solution)/shard_map/psum | solution.py:320
  914.4 13.3 %all-gather.31.cloned.1.call-done = bf16[1024,1024]{1,0:T(8,128)(2,1)} async-done(((bf16[256,1024]{1,0:T(8,128)(2,1)}), bf16[1024,1024]{1,0:T(8,128)(2,1)}) %all-gather.31.cloned.1.call-update) | async-done | bytes 2097168 | tf_op jit(solution)/shard_map/all_gather | solution.py:270
  (229 shorter events, 183.4 us)
Async XLA Ops:
  8.0 61.8 %all-gather.33.cloned.1.call-start = ((), (), s32[]{:S(2)}) async-start(), calls=%async_computation.32 | async-start | bytes 2621440 | tf_op jit(solution)/shard_map/all_gather | solution.py:134
  21.9 94.1 %all-gather.17.cloned.1.call-start = ((), (), s32[]{:S(2)}) async-start(), calls=%async_computation.12 | async-start | bytes 2621440 | tf_op jit(solution)/shard_map/all_gather | solution.py:133
  45.0 186.0 %reduce-scatter.13.cloned.1.call-start = ((), (), s32[]{:S(2)}) async-start(), calls=%async_computation.13 | async-start | bytes 2621440 | tf_op jit(solution)/shard_map/reduce_scatter | solution.py:97
  69.8 128.1 %copy-start.15 = (bf16[256,1024]{1,0:T(8,128)(2,1)}, bf16[256,1024]{1,0:T(8,128)(2,1)S(1)}, u32[]{:S(2)}) copy-start(bf16[256,1024]{1,0:T(8,128)(2,1)S(1)} %all_gather.71) | copy-start | bytes 1572868
  200.9 36.0 %all-gather.21.cloned.1.call-start = ((), (), s32[]{:S(2)}) async-start(), calls=%async_computation.15 | async-start | bytes 3145728 | tf_op jit(solution)/shard_map/all_gather | solution.py:77
  201.5 57.6 %all-gather.19.cloned.1.call-start = ((), (), s32[]{:S(2)}) async-start(), calls=%async_computation.14 | async-start | bytes 2621440 | tf_op jit(solution)/shard_map/all_gather | solution.py:102
  236.2 57.3 %all-gather.23.cloned.1.call-start = ((), (), s32[]{:S(2)}) async-start(), calls=%async_computation.16 | async-start | bytes 3145728 | tf_op jit(solution)/shard_map/all_gather | solution.py:78
  236.8 94.0 %reduce-scatter.15.cloned.1.call-start = ((), (), s32[]{:S(2)}) async-start(), calls=%async_computation.17 | async-start | bytes 2621440 | tf_op jit(solution)/shard_map/reduce_scatter | solution.py:97
  293.5 37.3 %copy-start = (bf16[256,1024]{1,0:T(8,128)(2,1)S(1)}, bf16[256,1024]{1,0:T(8,128)(2,1)}, u32[]{:S(2)}) copy-start(bf16[256,1024]{1,0:T(8,128)(2,1)} %reduce-scatter.13.cloned.1.call-done) | copy-start | bytes 1572868
  299.5 60.6 %all-gather.27.cloned.1.call-start = ((), (), s32[]{:S(2)}) async-start(), calls=%async_computation.19 | async-start | bytes 2621440 | tf_op jit(solution)/shard_map/all_gather | solution.py:102
  337.4 65.5 %reduce-scatter.17.cloned.1.call-start = ((), (), s32[]{:S(2)}) async-start(), calls=%async_computation.20 | async-start | bytes 2621440 | tf_op jit(solution)/shard_map/reduce_scatter | solution.py:97
  371.5 59.3 %all-gather.29.cloned.1.call-start = ((), (), s32[]{:S(2)}) async-start(), calls=%async_computation.21 | async-start | bytes 2621440 | tf_op jit(solution)/shard_map/all_gather | solution.py:102
  408.1 200.0 %reduce-scatter.19.cloned.1.call-start = ((), (), s32[]{:S(2)}) async-start(), calls=%async_computation.22 | async-start | bytes 2621440 | tf_op jit(solution)/shard_map/reduce_scatter | solution.py:232
  490.4 41.9 %copy-start.4 = (bf16[1,4096,4,64]{1,3,2,0:T(8,128)(2,1)S(1)}, bf16[1,4096,4,64]{1,3,2,0:T(8,128)(2,1)}, u32[]{:S(2)}) copy-start(bf16[1,4096,4,64]{1,3,2,0:T(8,128)(2,1)} %copy-done.3) | copy-start | bytes 6291460 | tf_op jit(solution)/shard_map/cond
  564.3 45.0 %copy-start.17 = (f32[1024,32]{0,1:T(8,128)S(1)}, f32[1024,32]{0,1:T(8,128)}, u32[]{:S(2)}) copy-start(f32[1024,32]{0,1:T(8,128)} %copy-done.16) | copy-start | bytes 393220
  564.3 45.0 %copy-start.22 = (f32[1024,32]{0,1:T(8,128)S(1)}, f32[1024,32]{0,1:T(8,128)}, u32[]{:S(2)}) copy-start(f32[1024,32]{0,1:T(8,128)} %get-tuple-element.168) | copy-start | bytes 393220
  564.3 47.1 %copy-start.11 = (bf16[1,1024,1024]{2,1,0:T(8,128)(2,1)S(1)}, bf16[1,1024,1024]{2,1,0:T(8,128)(2,1)}, u32[]{:S(2)}) copy-start(bf16[1,1024,1024]{2,1,0:T(8,128)(2,1)} %param.18) | copy-start | bytes 6291460
  564.3 89.5 %reduce-scatter.21.cloned.1.call-start = ((), (), s32[]{:S(2)}) async-start(), calls=%async_computation.23 | async-start | bytes 2621440 | tf_op jit(solution)/shard_map/reduce_scatter | solution.py:235
  565.1 105.4 %reduce-scatter.25.cloned.1.call-start = ((), (), s32[]{:S(2)}) async-start(), calls=%async_computation.26 | async-start | bytes 786432 | tf_op jit(solution)/shard_map/reduce_scatter | solution.py:285
  612.9 92.3 %reduce-scatter.33.cloned.1.call-start = ((), (), s32[]{:S(2)}) async-start(), calls=%async_computation.30 | async-start | bytes 3145728 | tf_op jit(solution)/shard_map/reduce_scatter | solution.py:297
  618.9 120.9 %reduce-scatter.35.cloned.1.call-start = ((), (), s32[]{:S(2)}) async-start(), calls=%async_computation.31 | async-start | bytes 3145728 | tf_op jit(solution)/shard_map/reduce_scatter | solution.py:300
  625.0 131.8 %reduce-scatter.31.cloned.1.call-start = ((), (), s32[]{:S(2)}) async-start(), calls=%async_computation.29 | async-start | bytes 786432 | tf_op jit(solution)/shard_map/reduce_scatter | solution.py:294
  628.2 145.9 %reduce-scatter.29.cloned.1.call-start = ((), (), s32[]{:S(2)}) async-start(), calls=%async_computation.28 | async-start | bytes 786432 | tf_op jit(solution)/shard_map/reduce_scatter | solution.py:291
  657.2 134.4 %reduce-scatter.27.cloned.1.call-start = ((), (), s32[]{:S(2)}) async-start(), calls=%async_computation.27 | async-start | bytes 786432 | tf_op jit(solution)/shard_map/reduce_scatter | solution.py:288
  660.5 165.3 %reduce-scatter.23.cloned.1.call-start = ((), (), s32[]{:S(2)}) async-start(), calls=%async_computation.24 | async-start | bytes 2621440 | tf_op jit(solution)/shard_map/reduce_scatter | solution.py:97
  664.2 161.6 %copy-start.12 = (f32[256,1024]{1,0:T(8,128)S(1)}, f32[256,1024]{1,0:T(8,128)}, u32[]{:S(2)}) copy-start(f32[256,1024]{1,0:T(8,128)} %get-tuple-element.146) | copy-start | bytes 3145732
  664.2 164.8 %copy-start.36 = (u32[32]{0:T(128)S(1)}, u32[32]{0:T(128)}, u32[]{:S(2)}) copy-start(u32[32]{0:T(128)} %constant.142) | copy-start | bytes 388
  664.2 166.0 %copy-start.27 = (bf16[1024]{0:T(1024)(128)(2,1)S(1)}, bf16[1024]{0:T(1024)(128)(2,1)}, u32[]{:S(2)}) copy-start(bf16[1024]{0:T(1024)(128)(2,1)} %get-tuple-element.117) | copy-start | bytes 6148
  664.2 166.0 %all-gather.25.cloned.1.call-start = ((), (), s32[]{:S(2)}) async-start(), calls=%async_computation.18 | async-start | bytes 2621440 | tf_op jit(solution)/shard_map/all_gather | solution.py:269
  665.0 194.3 %all-gather.35.cloned.1.call-start = ((), (), s32[]{:S(2)}) async-start(), calls=%async_computation.33 | async-start | bytes 1310720 | tf_op jit(solution)/shard_map/all_gather | solution.py:317
  670.5 233.7 %all-reduce.9.cloned.1.call-start = ((), (), s32[]{:S(2)}) async-start(), calls=%async_computation.34 | async-start | bytes 5767168 | tf_op jit(solution)/shard_map/psum | solution.py:320
  791.7 136.0 %all-gather.31.cloned.1.call-start = ((), (), s32[]{:S(2)}) async-start(), calls=%async_computation.25 | async-start | bytes 2621440 | tf_op jit(solution)/shard_map/all_gather | solution.py:270
  (29 other events, 253.4 us)
Sparse Core Ops, SparseCore 0:
  22.0 47.3 all-gather.32
  71.5 44.4 all-gather.16
  201.0 29.9 reduce-scatter.12
  337.5 22.5 all-gather.26
  408.2 22.5 all-gather.28
  564.4 43.6 reduce-scatter.18
  611.0 42.8 reduce-scatter.20
  656.7 13.8 reduce-scatter.24
  673.3 31.8 reduce-scatter.32
  707.9 31.8 reduce-scatter.34
  742.1 14.6 reduce-scatter.30
  759.5 14.6 reduce-scatter.28
  776.9 14.6 reduce-scatter.26
  794.6 31.1 reduce-scatter.22
Sparse Core Ops, SparseCore 1:
  202.9 31.7 all-gather.20
  236.7 22.4 all-gather.18
  260.6 32.9 all-gather.22
  299.6 31.2 reduce-scatter.14
  371.6 31.2 reduce-scatter.16
  667.2 21.6 all-gather.24
  690.2 27.9 all-gather.34
  791.7 112.5 all-reduce.8
  906.3 21.3 all-gather.30
